TPU v7x, 512 devices: a whole 4x4x16 slice. The times are simulated.
512 devices in a mesh: req: 32 (over z, core), mlp: 16 (over y, x).
Axes of the slice: x: 4, y: 4, z: 16, core: 2. Of those that a mesh axis runs over, the one named last changes fastest.
Arguments:
- hidden_input: bfloat16 [12288, 4096], P('req', 'mlp'), may hold values from -6 to 6
- input_norm_gain: bfloat16 [4096], replicated, may hold values from 0.099609375 to 1.8984375
- query_norm_gain: bfloat16 [128], replicated, may hold values from 0.099609375 to 1.8984375
- key_norm_gain: bfloat16 [128], replicated, may hold values from 0.099609375 to 1.8984375
- query_weight: bfloat16 [4096, 4096], P('req', 'mlp'), may hold values from -0.09375 to 0.09375
- key_value_weight: bfloat16 [4096, 2, 1024], P('req'), may hold values from -0.09375 to 0.09375
- output_weight: bfloat16 [4096, 16, 256], P('mlp', None, 'req'), may hold values from -0.09375 to 0.09375
- adapter_down_qkv: bfloat16 [64, 48, 4096], P('req', None, 'mlp'), may hold values from -0.09375 to 0.09375
- adapter_down_output: bfloat16 [64, 16, 4096], P('req', None, 'mlp'), may hold values from -0.09375 to 0.09375
- adapter_up_query: bfloat16 [64, 16, 4096], P('req', None, 'mlp'), may hold values from -1.5 to 1.5
- adapter_up_key_value: bfloat16 [64, 16, 2, 1024], P('req'), may hold values from -1.5 to 1.5
- adapter_up_output: bfloat16 [64, 16, 4096], P('req', None, 'mlp'), may hold values from -1.5 to 1.5
- pool: bfloat16 [16384, 2, 1024], P('req'), may hold values from -6 to 6
- lengths: int32 [32, 4], P('req'), may hold values from 1 to 192, 384 in all within a row
- cached_prefix_pages: int32 [32, 4], P('req'), may hold values from 0 to 8
- prefix_page_table: int32 [32, 4, 8], P('req'), may hold values from 0 to 7, each once within a row
- adapter_of_request: int32 [32, 4, 1], P('req'), may hold values from 0 to 63
- adapter_storage: int32 [64], replicated, may hold values from 0 to 63, each once
Outputs:
- attention_update: bfloat16 [12288, 4096], P('req', 'mlp')
- new_cache: bfloat16 [12288, 2, 1024], P('req', None, 'mlp')
Inputs may be any that keep to these rules, and one draw needn't show every extreme that they name: The lengths of one index of req sum to 384, and the longest of them is 192. `prefix_page_table`: each row lists every page of its pool once. `adapter_of_request`: every adapter is used by some request. `adapter_storage`: each slot holds one adapter.
All inputs are finite; a program needn't handle non-finite values.
Results may differ from a plain program's by a relative error of at most 0.035.
Values may be sent and summed in bfloat16 or wider, within the bound.
A program may use at most 64 MiB of HBM per device.

v0:
```python
import math
import jax
import jax.numpy as jnp
from jax import lax
from jax.sharding import PartitionSpec as P

QUERY_HEADS = 32
KEY_VALUE_HEADS = 8
HEAD_SIZE = 128
ADAPTER_RANK = 16
PAGE = 64
epsilon = 1e-06
rope_base = 1000000.0


def root_mean_scale(values, gain_vec):
    mean_sq = jnp.mean(values * values, axis=-1, keepdims=True)
    return values * lax.rsqrt(mean_sq + epsilon) * gain_vec.astype(jnp.float32)


def rotary_embed(values, token_positions):
    half_width = values.shape[-1] // 2
    inverse_freq = jnp.exp(
        jnp.arange(half_width, dtype=jnp.float32) * (-2.0 / values.shape[-1]) * math.log(rope_base)
    )
    angles = token_positions.astype(jnp.float32)[:, None] * inverse_freq[None, :]
    cosine = jnp.cos(angles)[:, None, :]
    sine_part = jnp.sin(angles)[:, None, :]
    front = values[..., :half_width]
    back = values[..., half_width:]
    return jnp.concatenate(
        [front * cosine - back * sine_part, back * cosine + front * sine_part], axis=-1
    )


def row_tables(lengths_row, prefix_row, page_rows, row_count):
    ends_at = jnp.cumsum(lengths_row)
    starts_at = ends_at - lengths_row
    row_ids = jnp.arange(row_count, dtype=jnp.int32)
    owners = jnp.sum((row_ids[:, None] >= ends_at[None, :]).astype(jnp.int32), axis=1)
    group_members = owners[:, None] == jnp.arange(lengths_row.shape[0], dtype=jnp.int32)[None, :]
    offsets = PAGE * prefix_row[None, :] + row_ids[:, None] - starts_at[None, :]
    token_positions = jnp.sum(jnp.where(group_members, offsets, 0), axis=1)
    page_ids = jnp.arange(page_rows.shape[1], dtype=jnp.int32)
    listed = (page_rows[:, :, None] == page_ids[None, None, :]) & (
        page_ids[None, :, None] < prefix_row[:, None, None]
    )
    page_used = jnp.sum(listed.astype(jnp.float32), axis=1)
    return (owners, group_members, token_positions, page_used)


def apply_adapter(lowrank_inner, group_members, chosen_up):
    masked = lowrank_inner[:, None, :] * group_members.astype(lowrank_inner.dtype)[:, :, None]
    return jnp.einsum("gjr,jrc->gc", masked, chosen_up, preferred_element_type=jnp.float32)


def select_rows(terms, group_members):
    return jnp.sum(terms * group_members.astype(jnp.float32)[:, :, None], axis=1)


def shards(
    hidden_input,
    input_norm_gain,
    query_norm_gain,
    key_norm_gain,
    query_weight,
    key_value_weight,
    output_weight,
    adapter_down_qkv,
    adapter_down_output,
    adapter_up_query,
    adapter_up_key_value,
    adapter_up_output,
    pool,
    lengths,
    cached_prefix_pages,
    prefix_page_table,
    adapter_of_request,
    adapter_storage,
):
    feature_group_count = lax.axis_size("mlp")
    feature_group_index = lax.axis_index("mlp")
    whole = lax.all_gather(hidden_input, "mlp", axis=1, tiled=True)
    row_count, full_width = whole.shape
    normalized_input = root_mean_scale(whole.astype(jnp.float32), input_norm_gain).astype(
        jnp.bfloat16
    )
    owners, group_members, token_positions, page_used = row_tables(
        lengths[0], cached_prefix_pages[0], prefix_page_table[0], row_count
    )
    q_width = query_weight.shape[1]
    query_head_rows = q_width // HEAD_SIZE
    key_value_local = max(1, KEY_VALUE_HEADS // feature_group_count)
    key_value_width = key_value_local * HEAD_SIZE
    key_value_begin = (
        feature_group_index * query_head_rows // (QUERY_HEADS // KEY_VALUE_HEADS) * HEAD_SIZE
    )
    own_wkv = lax.dynamic_slice_in_dim(key_value_weight, key_value_begin, key_value_width, 2)
    request_key_value_up = lax.dynamic_slice_in_dim(
        adapter_up_key_value, key_value_begin, key_value_width, 3
    )
    gathered = (
        lax.all_gather(adapter_down_qkv, "req", axis=0, tiled=True),
        lax.all_gather(adapter_down_output, "req", axis=0, tiled=True),
        lax.all_gather(adapter_up_query, "req", axis=0, tiled=True),
        lax.all_gather(request_key_value_up, "req", axis=0, tiled=True),
        lax.all_gather(adapter_up_output, "req", axis=0, tiled=True),
    )
    slot_indices = jnp.take(adapter_storage, adapter_of_request[0, :, 0], axis=0)
    chosen_down = jnp.take(gathered[0], slot_indices, axis=0)
    output_down = jnp.take(gathered[1], slot_indices, axis=0)
    query_up_part = jnp.take(gathered[2], slot_indices, axis=0)
    key_value_up = jnp.take(gathered[3], slot_indices, axis=0)
    output_up = jnp.take(gathered[4], slot_indices, axis=0)
    feature_cols = full_width // feature_group_count
    own_normed = lax.dynamic_slice_in_dim(
        normalized_input, feature_group_index * feature_cols, feature_cols, 1
    )
    low_terms = jnp.einsum(
        "gd,jkd->gjk", own_normed, chosen_down, preferred_element_type=jnp.float32
    )
    lowrank_inner = lax.psum(select_rows(low_terms, group_members).astype(jnp.bfloat16), "mlp")
    q_part = lax.all_gather(query_weight, "req", axis=0, tiled=True)
    kv_part = lax.all_gather(own_wkv, "req", axis=0, tiled=True)
    query_width_total = jnp.dot(normalized_input, q_part, preferred_element_type=jnp.float32)
    kv_total = jnp.dot(
        normalized_input,
        kv_part.reshape(kv_part.shape[0], 2 * key_value_width),
        preferred_element_type=jnp.float32,
    )
    query_width_total, kv_total = (query_width_total, kv_total)
    query_plain = (
        query_width_total
        + apply_adapter(lowrank_inner[:, 0:ADAPTER_RANK], group_members, query_up_part)
    ).astype(jnp.bfloat16)
    key_lowrank_part = apply_adapter(
        lowrank_inner[:, ADAPTER_RANK : 2 * ADAPTER_RANK], group_members, key_value_up[:, :, 0]
    )
    value_lowrank_part = apply_adapter(
        lowrank_inner[:, 2 * ADAPTER_RANK : 3 * ADAPTER_RANK], group_members, key_value_up[:, :, 1]
    )
    key_value_plain = (
        kv_total.reshape(row_count, 2, key_value_width)
        + jnp.stack([key_lowrank_part, value_lowrank_part], axis=1)
    ).astype(jnp.bfloat16)
    cached = lax.dynamic_slice_in_dim(pool, key_value_begin, key_value_width, 2)
    pool_token_rows = cached.shape[0]
    query_rotated = rotary_embed(
        root_mean_scale(
            query_plain.astype(jnp.float32).reshape(row_count, query_head_rows, HEAD_SIZE),
            query_norm_gain,
        ),
        token_positions,
    ).astype(jnp.bfloat16)
    key_rotated = rotary_embed(
        root_mean_scale(
            key_value_plain[:, 0]
            .astype(jnp.float32)
            .reshape(row_count, key_value_local, HEAD_SIZE),
            key_norm_gain,
        ),
        token_positions,
    ).astype(jnp.bfloat16)
    cache_columns = KEY_VALUE_HEADS * HEAD_SIZE // feature_group_count
    own_offset = feature_group_index * cache_columns - key_value_begin
    local_cache = jnp.stack(
        [key_rotated.reshape(row_count, key_value_width), key_value_plain[:, 1]], axis=1
    )
    new_cache = lax.dynamic_slice_in_dim(local_cache, own_offset, cache_columns, 2)
    key_matrix = jnp.concatenate(
        [cached[:, 0].reshape(pool_token_rows, key_value_local, HEAD_SIZE), key_rotated], axis=0
    )
    value_matrix = jnp.concatenate(
        [
            cached[:, 1].reshape(pool_token_rows, key_value_local, HEAD_SIZE),
            key_value_plain[:, 1].reshape(row_count, key_value_local, HEAD_SIZE),
        ],
        axis=0,
    )
    pool_ok = jnp.dot(group_members.astype(jnp.float32), page_used, precision=lax.Precision.HIGHEST)
    pool_ok = jnp.repeat(pool_ok, PAGE, axis=1) > 0.5
    row_ids = jnp.arange(row_count, dtype=jnp.int32)
    causal = (owners[:, None] == owners[None, :]) & (row_ids[None, :] <= row_ids[:, None])
    allowed = jnp.concatenate([pool_ok, causal], axis=1)
    query_rows = query_rotated.reshape(
        row_count, key_value_local, query_head_rows // key_value_local, HEAD_SIZE
    )
    scores = jnp.einsum(
        "gkhd,skd->khgs", query_rows, key_matrix, preferred_element_type=jnp.float32
    ) / math.sqrt(HEAD_SIZE)
    exp_scores = jnp.where(allowed[None, None], jnp.exp(scores), 0.0)
    softmax = (exp_scores / jnp.sum(exp_scores, axis=-1, keepdims=True)).astype(jnp.bfloat16)
    attended = jnp.einsum(
        "khgs,skd->gkhd", softmax, value_matrix, preferred_element_type=jnp.float32
    )
    attended = attended.astype(jnp.bfloat16).reshape(row_count, q_width)
    out_terms = jnp.einsum("gc,jrc->gjr", attended, output_down, preferred_element_type=jnp.float32)
    lowrank_result = lax.psum(select_rows(out_terms, group_members), "mlp").astype(jnp.bfloat16)
    partial_value = jnp.einsum(
        "gc,cnk->gnk",
        attended,
        lax.all_gather(output_weight, "req", axis=2, tiled=True),
        preferred_element_type=jnp.float32,
    )
    summed_output = lax.psum_scatter(
        partial_value.reshape(row_count, full_width).astype(jnp.bfloat16),
        "mlp",
        scatter_dimension=1,
        tiled=True,
    ).astype(jnp.float32)
    attention_update = (
        summed_output + apply_adapter(lowrank_result, group_members, output_up)
    ).astype(jnp.bfloat16)
    return (attention_update, new_cache)


def solution(mesh):
    return jax.shard_map(
        shards,
        mesh=mesh,
        in_specs=(
            P("req", "mlp"),
            P(),
            P(),
            P(),
            P("req", "mlp"),
            P("req", None, None),
            P("mlp", None, "req"),
            P("req", None, "mlp"),
            P("req", None, "mlp"),
            P("req", None, "mlp"),
            P("req", None, None, None),
            P("req", None, "mlp"),
            P("req", None, None),
            P("req", None),
            P("req", None),
            P("req", None, None),
            P("req", None, None),
            P(),
        ),
        out_specs=(P("req", "mlp"), P("req", None, "mlp")),
        check_vma=False,
    )
```

profile of v0, /device:TPU:32, one launch (start us, length us, event | category | flops | bytes accessed | tf_op | source)
XLA Modules:
  0.0 518.9 jit_solution(2938642543624137017)
XLA Ops:
  11.6 1.3 gather_fusion
  14.2 0.8 reduce-window.4
  16.5 0.7 constant_dynamic-slice_fusion.1
  17.3 36.1 %all_gather.30 = bf16[64,16,2,128]{3,1,2,0:T(8,128)(2,1)S(1)} all-gather(bf16[2,16,2,128]{3,1,2,0:T(8,128)(2,1)S(1)} %copy.66), channel_id=1, replica_groups=mesh['req'=32,'mlp'=16] {'req'}, dimensions={0}, use_global_device_ids=true | all-gather | bytes 540672 | tf_op jit(solution)/shard_map/all_gather | solution.py:106
  53.3 0.7 convert_element_type.100
  54.0 1.2 convert_element_type.109
  56.0 1.6 constant_dynamic-slice_fusion
  57.6 30.2 %all_gather.32 = bf16[64,16,256]{2,1,0:T(8,128)(2,1)S(1)} all-gather(bf16[2,16,256]{2,1,0:T(8,128)(2,1)S(1)} %copy-done.6), channel_id=1, replica_groups=mesh['req'=32,'mlp'=16] {'req'}, dimensions={0}, use_global_device_ids=true | all-gather | bytes 540672 | tf_op jit(solution)/shard_map/all_gather | solution.py:105
  90.7 1.2 gather_fusion.3
  91.8 0.8 multiply_cosine_fusion
  92.8 2.6 gather_fusion.1
  95.4 61.2 %all-gather.8.cloned.1.call-done = bf16[4096,2,128]{2,1,0:T(2,128)(2,1)} async-done(((bf16[128,2,128]{2,1,0:T(2,128)(2,1)}), bf16[4096,2,128]{2,1,0:T(2,128)(2,1)}) %all-gather.8.cloned.1.call-update) | async-done | bytes 2097168 | tf_op jit(solution)/shard_map/all_gather | solution.py:124
  156.6 4.7 copy.61
  161.3 63.1 %all-gather.6.cloned.1.call-done = bf16[384,4096]{1,0:T(8,128)(2,1)} async-done(((bf16[384,256]{1,0:T(8,128)(2,1)}), bf16[384,4096]{1,0:T(8,128)(2,1)}) %all-gather.6.cloned.1.call-update) | async-done | bytes 3145744 | tf_op jit(solution)/shard_map/all_gather | solution.py:83
  224.4 2.7 fusion
  227.3 1.1 fusion.2
  228.4 1.6 copy-done.2
  230.0 0.9 fusion.26
  230.9 72.8 %psum.14 = bf16[384,48]{0,1:T(8,128)(2,1)S(1)} all-reduce(bf16[384,48]{0,1:T(8,128)(2,1)} %fusion.26), channel_id=1, replica_groups=mesh['req'=32,'mlp'=16] {'mlp'}, use_global_device_ids=true, to_apply=%region_4.5 | all-reduce | flops 18432 | bytes 73728 | tf_op jit(solution)/shard_map/psum | solution.py:122
  303.7 0.9 convolution_bitcast_fusion.2
  304.7 0.9 convolution_bitcast_fusion.3
  305.6 3.2 fusion.17
  309.6 3.8 fusion.92
  314.5 0.9 fusion.5
  315.5 0.9 fusion.23
  316.4 53.5 %all-gather.14.cloned.1.call-done = bf16[256,16,256]{0,2,1:T(8,128)(2,1)} async-done(((bf16[256,16,8]{0,2,1:T(8,128)(2,1)}), bf16[256,16,256]{0,2,1:T(8,128)(2,1)}) %all-gather.14.cloned.1.call-update) | async-done | bytes 2097168 | tf_op jit(solution)/shard_map/all_gather | solution.py:202
  369.9 4.3 convolution_convert_fusion
  374.9 28.9 %all_gather.34 = bf16[64,16,256]{2,1,0:T(8,128)(2,1)S(1)} all-gather(bf16[2,16,256]{2,1,0:T(8,128)(2,1)S(1)} %copy-done.7), channel_id=1, replica_groups=mesh['req'=32,'mlp'=16] {'req'}, dimensions={0}, use_global_device_ids=true | all-gather | bytes 540672 | tf_op jit(solution)/shard_map/all_gather | solution.py:104
  404.3 30.1 %all_gather.35 = bf16[64,16,256]{2,1,0:T(8,128)(2,1)S(1)} all-gather(bf16[2,16,256]{2,1,0:T(8,128)(2,1)S(1)} %copy-done.8), channel_id=1, replica_groups=mesh['req'=32,'mlp'=16] {'req'}, dimensions={0}, use_global_device_ids=true | all-gather | bytes 540672 | tf_op jit(solution)/shard_map/all_gather | solution.py:107
  435.2 74.3 %psum.15 = bf16[384,16]{0,1:T(8,128)(2,1)S(1)} all-reduce(f32[384,16]{0,1:T(8,128)S(1)} %fusion.27), channel_id=1, replica_groups=mesh['req'=32,'mlp'=16] {'mlp'}, use_global_device_ids=true, to_apply=%region_12.14 | all-reduce | flops 6144 | bytes 36864 | tf_op jit(solution)/shard_map/psum | solution.py:198
  509.5 0.7 fusion.50
  510.2 1.9 fusion.16
  (94 shorter events, 14.7 us)
Async XLA Ops:
  7.2 1.1 copy-start
  7.2 81.2 %copy-start.17 = (s32[1,4]{1,0:T(1,128)S(1)}, s32[1,4]{1,0:T(1,128)}, u32[]{:S(2)}) copy-start(s32[1,4]{1,0:T(1,128)} %param.34) | copy-start | bytes 52
  7.2 50.4 %copy-start.6 = (bf16[2,16,256]{2,1,0:T(8,128)(2,1)S(1)}, bf16[2,16,256]{2,1,0:T(8,128)(2,1)}, u32[]{:S(2)}) copy-start(bf16[2,16,256]{2,1,0:T(8,128)(2,1)} %param.29) | copy-start | bytes 49156
  7.2 80.6 %copy-start.16 = (bf16[128]{0:T(256)(128)(2,1)S(1)}, bf16[128]{0:T(256)(128)(2,1)}, u32[]{:S(2)}) copy-start(bf16[128]{0:T(256)(128)(2,1)} %param.22) | copy-start | bytes 772
  7.2 81.2 %copy-start.13 = (s32[1,4,8]{2,1,0:T(4,128)S(1)}, s32[1,4,8]{2,1,0:T(4,128)}, u32[]{:S(2)}) copy-start(s32[1,4,8]{2,1,0:T(4,128)} %param.35) | copy-start | bytes 388
  7.2 85.5 %all-gather.10.cloned.1.call-start = ((), (), s32[]{:S(2)}) async-start(), calls=%async_computation.3 | async-start | bytes 1622016 | tf_op jit(solution)/shard_map/all_gather | solution.py:103
  8.0 148.6 %all-gather.8.cloned.1.call-start = ((), (), s32[]{:S(2)}) async-start(), calls=%async_computation.2 | async-start | bytes 2162688 | tf_op jit(solution)/shard_map/all_gather | solution.py:124
  8.9 215.5 %all-gather.6.cloned.1.call-start = ((), (), s32[]{:S(2)}) async-start(), calls=%async_computation.1 | async-start | bytes 3342336 | tf_op jit(solution)/shard_map/all_gather | solution.py:83
  9.7 299.9 %all-gather.12.cloned.1.call-start = ((), (), s32[]{:S(2)}) async-start(), calls=%async_computation.4 | async-start | bytes 2162688 | tf_op jit(solution)/shard_map/all_gather | solution.py:123
  10.3 359.6 %all-gather.14.cloned.1.call-start = ((), (), s32[]{:S(2)}) async-start(), calls=%async_computation.5 | async-start | bytes 2162688 | tf_op jit(solution)/shard_map/all_gather | solution.py:202
  10.8 499.4 %reduce-scatter.2.cloned.1.call-start = ((), (), s32[]{:S(2)}) async-start(), calls=%async_computation.6 | async-start | bytes 3342336 | tf_op jit(solution)/shard_map/reduce_scatter | solution.py:205
  14.2 147.1 %copy-start.11 = (f32[64]{0:T(128)}, f32[64]{0:T(128)S(1)}, u32[]{:S(2)}) copy-start(f32[64]{0:T(128)S(1)} %multiply_exponential_fusion) | copy-start | bytes 772
  224.4 2.8 copy-start.1
  227.3 2.8 copy-start.5
  227.3 2.8 copy-start.9
  228.4 1.7 copy-start.2
  305.6 3.3 copy-start.14
  305.6 3.4 copy-start.12
  309.6 3.9 copy-start.4
  309.6 4.5 copy-start.15
  314.3 1.2 copy-start.3
  374.1 0.7 copy-start.7
  374.1 30.2 %copy-start.8 = (bf16[2,16,256]{2,1,0:T(8,128)(2,1)S(1)}, bf16[2,16,256]{2,1,0:T(8,128)(2,1)}, u32[]{:S(2)}) copy-start(bf16[2,16,256]{2,1,0:T(8,128)(2,1)} %param.31) | copy-start | bytes 49156
  374.1 60.9 %copy-start.10 = (f32[384,4]{0,1:T(4,128)S(1)}, f32[384,4]{0,1:T(4,128)}, u32[]{:S(2)}) copy-start(f32[384,4]{0,1:T(4,128)} %get-tuple-element.17) | copy-start | bytes 18436
Sparse Core Ops, SparseCore 0:
  10.2 75.3 all-gather.9
  87.7 68.8 all-gather.7
  159.6 64.8 all-gather.5
  226.4 71.1 all-gather.11
  299.5 70.3 all-gather.13
  374.3 87.2 reduce-scatter.1
where the time goes:
time: 520 us; the launch traced here: 519 us
  blocking collectives  272 us (52%)
  waiting for transfers between devices  180 us (35%)
  matrix products  18.5 us (4%)
  local copies, waits for them, and re-layouts  18.3 us (4%)
  other arithmetic  14.7 us (3%)
  between operations  14.6 us (3%)
    psum x1, blocking collectives, shards(): lax.psum(select_rows(out_terms, group_members), 'mlp').astype(jnp.bfloat16)  74.3 us
    psum x1, blocking collectives, shards(): lax.psum(select_rows(low_terms, group_members).astype(jnp.bfloat16), 'mlp')  72.8 us
    all_gather x1, waiting for transfers between devices, shards(): whole = lax.all_gather(hidden_input, 'mlp', axis=1, tiled=True)  63.1 us
    all_gather x1, waiting for transfers between devices, shards(): kv_part = lax.all_gather(own_wkv, 'req', axis=0, tiled=True)  61.2 us
    all_gather x1, waiting for transfers between devices, shards(): lax.all_gather(output_weight, 'req', axis=2, tiled=True)  53.5 us
    all_gather x1, blocking collectives, shards(): lax.all_gather(request_key_value_up, 'req', axis=0, tiled=True)  36.1 us
    all_gather x1, blocking collectives, shards(): lax.all_gather(adapter_up_query, 'req', axis=0, tiled=True)  30.2 us
    all_gather x1, blocking collectives, shards(): lax.all_gather(adapter_up_output, 'req', axis=0, tiled=True)  30.1 us
  transfers between devices with their start and end apart: 6, of which 3 were waited for; matrix products, arithmetic and copies ran while one was open for 8% of the time, Pallas kernels for 0%

commit v1 on v0

--- a/solution.py
+++ b/solution.py
@@ -80,7 +80,12 @@
 ):
     feature_group_count = lax.axis_size("mlp")
     feature_group_index = lax.axis_index("mlp")
-    whole = lax.all_gather(hidden_input, "mlp", axis=1, tiled=True)
+    ring = [hidden_input]
+    for hop in range(15):
+        ring.append(lax.ppermute(ring[-1], "mlp", [(dev, (dev + 1) % 16) for dev in range(16)]))
+    whole = jnp.roll(
+        jnp.concatenate(ring[::-1], axis=1), (lax.axis_index("mlp") + 1) * ring[0].shape[1], axis=1
+    )
     row_count, full_width = whole.shape
     normalized_input = root_mean_scale(whole.astype(jnp.float32), input_norm_gain).astype(
         jnp.bfloat16

time: 520 us -> 466 us (0.90)
  waiting for transfers between devices: 180 us -> 104 us
  starting transfers between devices: 0.23 us -> 30.3 us
  blocking collectives: 272 us -> 264 us
    ppermute x0 -> x15, waiting for transfers between devices: none -> 103 us  [shards(): lax.ppermute(ring[-1], 'mlp', [(dev, (dev + 1) % 16) for dev in range(16)])]
    all_gather x1 -> x0, waiting for transfers between devices: 63.1 us -> none  [shards(): whole = lax.all_gather(hidden_input, 'mlp', axis=1, tiled=True)]
    all_gather x1, waiting for transfers between devices: 61.2 us -> 0.01 us  [shards(): kv_part = lax.all_gather(own_wkv, 'req', axis=0, tiled=True)]
    all_gather x1, waiting for transfers between devices: 53.5 us -> 0.02 us  [shards(): lax.all_gather(output_weight, 'req', axis=2, tiled=True)]
    ppermute x0 -> x15, starting transfers between devices: none -> 30.1 us  [shards(): lax.ppermute(ring[-1], 'mlp', [(dev, (dev + 1) % 16) for dev in range(16)])]
  transfers between devices with their start and end apart: 6 -> 20, of which waited for: 3 -> 13; matrix products, arithmetic and copies ran while one was open for 8% -> 10% of each run, Pallas kernels for 0% -> 0%
where the time goes in v1:
time: 466 us; the launch traced here: 465 us
  blocking collectives  264 us (57%)
  waiting for transfers between devices  104 us (22%)
  starting transfers between devices  30.3 us (7%)
  matrix products  18.8 us (4%)
  other arithmetic  17.2 us (4%)
  local copies, waits for them, and re-layouts  15.8 us (3%)
  between operations  14.6 us (3%)
    ppermute x15, waiting for transfers between devices, shards(): lax.ppermute(ring[-1], 'mlp', [(dev, (dev + 1) % 16) for dev in range(16)])  103 us
    psum x1, blocking collectives, shards(): lax.psum(select_rows(low_terms, group_members).astype(jnp.bfloat16), 'mlp')  69.8 us
    psum x1, blocking collectives, shards(): lax.psum(select_rows(out_terms, group_members), 'mlp').astype(jnp.bfloat16)  69.6 us
    all_gather x1, blocking collectives, shards(): lax.all_gather(request_key_value_up, 'req', axis=0, tiled=True)  35.6 us
    all_gather x1, blocking collectives, shards(): lax.all_gather(adapter_up_query, 'req', axis=0, tiled=True)  30.6 us
    ppermute x15, starting transfers between devices, shards(): lax.ppermute(ring[-1], 'mlp', [(dev, (dev + 1) % 16) for dev in range(16)])  30.1 us
    all_gather x1, blocking collectives, shards(): lax.all_gather(adapter_up_output, 'req', axis=0, tiled=True)  29.6 us
    all_gather x1, blocking collectives, shards(): lax.all_gather(adapter_down_output, 'req', axis=0, tiled=True)  28.7 us
  transfers between devices with their start and end apart: 20, of which 13 were waited for; matrix products, arithmetic and copies ran while one was open for 10% of the time, Pallas kernels for 0%

profile of v1, /device:TPU:32, one launch (start us, length us, event | category | flops | bytes accessed | tf_op | source)
XLA Modules:
  0.0 465.1 jit_solution(3498082894791414444)
XLA Ops:
  9.7 3.4 collective-permute-start
  18.8 3.2 collective-permute-done
  21.9 1.9 collective-permute-start.1
  26.4 6.7 %collective-permute-done.1 = bf16[384,256]{1,0:T(8,128)(2,1)S(1)} collective-permute-done((bf16[384,256]{1,0:T(8,128)(2,1)S(1)}, bf16[384,256]{1,0:T(8,128)(2,1)S(1)}, u32[]{:S(2)}, u32[]{:S(2)}) %collective-permute-start.1) | collective-permute-done | bytes 196640 | tf_op jit(solution)/shard_map/ppermute | solution.py:85
  33.1 1.9 collective-permute-start.2
  35.6 8.3 %collective-permute-done.2 = bf16[384,256]{1,0:T(8,128)(2,1)S(1)} collective-permute-done((bf16[384,256]{1,0:T(8,128)(2,1)S(1)}, bf16[384,256]{1,0:T(8,128)(2,1)S(1)}, u32[]{:S(2)}, u32[]{:S(2)}) %collective-permute-start.2) | collective-permute-done | bytes 196640 | tf_op jit(solution)/shard_map/ppermute | solution.py:85
  48.2 6.6 %collective-permute-done.3 = bf16[384,256]{1,0:T(8,128)(2,1)S(1)} collective-permute-done((bf16[384,256]{1,0:T(8,128)(2,1)S(1)}, bf16[384,256]{1,0:T(8,128)(2,1)S(1)}, u32[]{:S(2)}, u32[]{:S(2)}) %collective-permute-start.3) | collective-permute-done | bytes 196640 | tf_op jit(solution)/shard_map/ppermute | solution.py:85
  54.8 1.9 collective-permute-start.4
  56.7 35.6 %all_gather.26 = bf16[64,16,2,128]{3,1,2,0:T(8,128)(2,1)S(1)} all-gather(bf16[2,16,2,128]{3,1,2,0:T(8,128)(2,1)S(1)} %copy.66), channel_id=1, replica_groups=mesh['req'=32,'mlp'=16] {'req'}, dimensions={0}, use_global_device_ids=true | all-gather | bytes 540672 | tf_op jit(solution)/shard_map/all_gather | solution.py:111
  92.9 1.9 collective-permute-start.5
  94.9 30.6 %all_gather.28 = bf16[64,16,256]{2,1,0:T(8,128)(2,1)S(1)} all-gather(bf16[2,16,256]{2,1,0:T(8,128)(2,1)} %param.29), channel_id=1, replica_groups=mesh['req'=32,'mlp'=16] {'req'}, dimensions={0}, use_global_device_ids=true | all-gather | bytes 540672 | tf_op jit(solution)/shard_map/all_gather | solution.py:110
  125.5 1.9 collective-permute-start.6
  128.1 10.1 %collective-permute-done.6 = bf16[384,256]{1,0:T(8,128)(2,1)S(1)} collective-permute-done((bf16[384,256]{1,0:T(8,128)(2,1)S(1)}, bf16[384,256]{1,0:T(8,128)(2,1)S(1)}, u32[]{:S(2)}, u32[]{:S(2)}) %collective-permute-start.6) | collective-permute-done | bytes 196640 | tf_op jit(solution)/shard_map/ppermute | solution.py:85
  138.1 1.9 collective-permute-start.7
  140.8 9.1 %collective-permute-done.7 = bf16[384,256]{1,0:T(8,128)(2,1)S(1)} collective-permute-done((bf16[384,256]{1,0:T(8,128)(2,1)S(1)}, bf16[384,256]{1,0:T(8,128)(2,1)S(1)}, u32[]{:S(2)}, u32[]{:S(2)}) %collective-permute-start.7) | collective-permute-done | bytes 196640 | tf_op jit(solution)/shard_map/ppermute | solution.py:85
  153.8 7.0 %collective-permute-done.8 = bf16[384,256]{1,0:T(8,128)(2,1)S(1)} collective-permute-done((bf16[384,256]{1,0:T(8,128)(2,1)S(1)}, bf16[384,256]{1,0:T(8,128)(2,1)S(1)}, u32[]{:S(2)}, u32[]{:S(2)}) %collective-permute-start.8) | collective-permute-done | bytes 196640 | tf_op jit(solution)/shard_map/ppermute | solution.py:85
  162.9 8.8 %collective-permute-done.9 = bf16[384,256]{1,0:T(8,128)(2,1)S(1)} collective-permute-done((bf16[384,256]{1,0:T(8,128)(2,1)S(1)}, bf16[384,256]{1,0:T(8,128)(2,1)S(1)}, u32[]{:S(2)}, u32[]{:S(2)}) %collective-permute-start.9) | collective-permute-done | bytes 196640 | tf_op jit(solution)/shard_map/ppermute | solution.py:85
  173.8 8.8 %collective-permute-done.10 = bf16[384,256]{1,0:T(8,128)(2,1)S(1)} collective-permute-done((bf16[384,256]{1,0:T(8,128)(2,1)S(1)}, bf16[384,256]{1,0:T(8,128)(2,1)S(1)}, u32[]{:S(2)}, u32[]{:S(2)}) %collective-permute-start.10) | collective-permute-done | bytes 196640 | tf_op jit(solution)/shard_map/ppermute | solution.py:85
  185.4 8.1 %collective-permute-done.11 = bf16[384,256]{1,0:T(8,128)(2,1)S(1)} collective-permute-done((bf16[384,256]{1,0:T(8,128)(2,1)S(1)}, bf16[384,256]{1,0:T(8,128)(2,1)S(1)}, u32[]{:S(2)}, u32[]{:S(2)}) %collective-permute-start.11) | collective-permute-done | bytes 196640 | tf_op jit(solution)/shard_map/ppermute | solution.py:85
  196.1 8.2 %collective-permute-done.12 = bf16[384,256]{1,0:T(8,128)(2,1)S(1)} collective-permute-done((bf16[384,256]{1,0:T(8,128)(2,1)S(1)}, bf16[384,256]{1,0:T(8,128)(2,1)S(1)}, u32[]{:S(2)}, u32[]{:S(2)}) %collective-permute-start.12) | collective-permute-done | bytes 196640 | tf_op jit(solution)/shard_map/ppermute | solution.py:85
  206.3 9.0 %collective-permute-done.13 = bf16[384,256]{1,0:T(8,128)(2,1)S(1)} collective-permute-done((bf16[384,256]{1,0:T(8,128)(2,1)S(1)}, bf16[384,256]{1,0:T(8,128)(2,1)S(1)}, u32[]{:S(2)}, u32[]{:S(2)}) %collective-permute-start.13) | collective-permute-done | bytes 196640 | tf_op jit(solution)/shard_map/ppermute | solution.py:85
  217.3 8.9 %collective-permute-done.14 = bf16[384,256]{1,0:T(8,128)(2,1)S(1)} collective-permute-done((bf16[384,256]{1,0:T(8,128)(2,1)S(1)}, bf16[384,256]{1,0:T(8,128)(2,1)S(1)}, u32[]{:S(2)}, u32[]{:S(2)}) %collective-permute-start.14) | collective-permute-done | bytes 196640 | tf_op jit(solution)/shard_map/ppermute | solution.py:85
  227.8 2.7 fusion.2
  230.5 2.0 gather_fusion.1
  233.6 69.8 %psum.14 = bf16[384,48]{0,1:T(8,128)(2,1)S(1)} all-reduce(bf16[384,48]{0,1:T(8,128)(2,1)S(1)} %fusion.25), channel_id=1, replica_groups=mesh['req'=32,'mlp'=16] {'mlp'}, use_global_device_ids=true, to_apply=%region_4.5 | all-reduce | flops 18432 | bytes 73728 | tf_op jit(solution)/shard_map/psum | solution.py:127
  305.6 4.7 %copy.61 = bf16[4096,2,128]{0,2,1:T(8,128)(2,1)S(1)} copy(bf16[4096,2,128]{2,1,0:T(2,128)(2,1)} %all-gather.5.cloned.1.call-done) | data formatting | bytes 4194304 | tf_op jit(solution)/shard_map/reshape | solution.py:133
  310.3 3.3 fusion.17
  315.9 3.9 multiply_reduce_fusion
  322.3 4.3 convolution_convert_fusion
  326.6 28.7 %all_gather.30 = bf16[64,16,256]{2,1,0:T(8,128)(2,1)S(1)} all-gather(bf16[2,16,256]{2,1,0:T(8,128)(2,1)S(1)} %copy-done.5), channel_id=1, replica_groups=mesh['req'=32,'mlp'=16] {'req'}, dimensions={0}, use_global_device_ids=true | all-gather | bytes 540672 | tf_op jit(solution)/shard_map/all_gather | solution.py:109
  355.9 29.6 %all_gather.31 = bf16[64,16,256]{2,1,0:T(8,128)(2,1)S(1)} all-gather(bf16[2,16,256]{2,1,0:T(8,128)(2,1)S(1)} %copy-done.6), channel_id=1, replica_groups=mesh['req'=32,'mlp'=16] {'req'}, dimensions={0}, use_global_device_ids=true | all-gather | bytes 540672 | tf_op jit(solution)/shard_map/all_gather | solution.py:112
  386.3 69.6 %psum.15 = bf16[384,16]{0,1:T(8,128)(2,1)S(1)} all-reduce(f32[384,16]{0,1:T(8,128)S(1)} %fusion.26), channel_id=1, replica_groups=mesh['req'=32,'mlp'=16] {'mlp'}, use_global_device_ids=true, to_apply=%region_12.14 | all-reduce | flops 6144 | bytes 36864 | tf_op jit(solution)/shard_map/psum | solution.py:203
  (139 shorter events, 48.0 us)
Async XLA Ops:
  7.2 1.0 copy-start
  7.2 219.4 %copy-start.1 = (bf16[384,256]{1,0:T(8,128)(2,1)S(1)}, bf16[384,256]{1,0:T(8,128)(2,1)}, u32[]{:S(2)}) copy-start(bf16[384,256]{1,0:T(8,128)(2,1)} %param.20) | copy-start | bytes 589828
  7.2 223.3 %all-gather.7.cloned.1.call-start = ((), (), s32[]{:S(2)}) async-start(), calls=%async_computation.2 | async-start | bytes 1622016 | tf_op jit(solution)/shard_map/all_gather | solution.py:108
  7.9 297.7 %all-gather.5.cloned.1.call-start = ((), (), s32[]{:S(2)}) async-start(), calls=%async_computation.1 | async-start | bytes 2162688 | tf_op jit(solution)/shard_map/all_gather | solution.py:129
  8.9 306.9 %all-gather.9.cloned.1.call-start = ((), (), s32[]{:S(2)}) async-start(), calls=%async_computation.3 | async-start | bytes 2162688 | tf_op jit(solution)/shard_map/all_gather | solution.py:128
  9.6 312.6 %all-gather.11.cloned.1.call-start = ((), (), s32[]{:S(2)}) async-start(), calls=%async_computation.4 | async-start | bytes 2162688 | tf_op jit(solution)/shard_map/all_gather | solution.py:207
  9.7 12.2 %collective-permute-start = (bf16[384,256]{1,0:T(8,128)(2,1)}, bf16[384,256]{1,0:T(8,128)(2,1)S(1)}, u32[]{:S(2)}, u32[]{:S(2)}) collective-permute-start(bf16[384,256]{1,0:T(8,128)(2,1)} %param.20), channel_id=1, source_target_pairs={{0,1},{1,2},{2,3},{3,4},{4,5},{5,6},{6,7},{7,8},{8,9},{9,10},{10,1... | collective-permute-start | bytes 589832 | tf_op jit(solution)/shard_map/ppermute | solution.py:85
  13.1 443.5 %reduce-scatter.2.cloned.1.call-start = ((), (), s32[]{:S(2)}) async-start(), calls=%async_computation.5 | async-start | bytes 3342336 | tf_op jit(solution)/shard_map/reduce_scatter | solution.py:210
  21.9 11.1 %collective-permute-start.1 = (bf16[384,256]{1,0:T(8,128)(2,1)S(1)}, bf16[384,256]{1,0:T(8,128)(2,1)S(1)}, u32[]{:S(2)}, u32[]{:S(2)}) collective-permute-start(bf16[384,256]{1,0:T(8,128)(2,1)S(1)} %collective-permute-done), channel_id=1, source_target_pairs={{0,1},{1,2},{2,3},{3,4},{4,5},{5,6},{6,7},{7,8},{8,9},{9,10},{10,1... | collective-permute-start | bytes 589832 | tf_op jit(solution)/shard_map/ppermute | solution.py:85
  33.1 10.9 %collective-permute-start.2 = (bf16[384,256]{1,0:T(8,128)(2,1)S(1)}, bf16[384,256]{1,0:T(8,128)(2,1)S(1)}, u32[]{:S(2)}, u32[]{:S(2)}) collective-permute-start(bf16[384,256]{1,0:T(8,128)(2,1)S(1)} %collective-permute-done.1), channel_id=1, source_target_pairs={{0,1},{1,2},{2,3},{3,4},{4,5},{5,6},{6,7},{7,8},{8,9},{9,10},{10,1... | collective-permute-start | bytes 589832 | tf_op jit(solution)/shard_map/ppermute | solution.py:85
  43.9 10.9 %collective-permute-start.3 = (bf16[384,256]{1,0:T(8,128)(2,1)S(1)}, bf16[384,256]{1,0:T(8,128)(2,1)S(1)}, u32[]{:S(2)}, u32[]{:S(2)}) collective-permute-start(bf16[384,256]{1,0:T(8,128)(2,1)S(1)} %collective-permute-done.2), channel_id=1, source_target_pairs={{0,1},{1,2},{2,3},{3,4},{4,5},{5,6},{6,7},{7,8},{8,9},{9,10},{10,1... | collective-permute-start | bytes 589832 | tf_op jit(solution)/shard_map/ppermute | solution.py:85
  54.8 38.1 %collective-permute-start.4 = (bf16[384,256]{1,0:T(8,128)(2,1)S(1)}, bf16[384,256]{1,0:T(8,128)(2,1)S(1)}, u32[]{:S(2)}, u32[]{:S(2)}) collective-permute-start(bf16[384,256]{1,0:T(8,128)(2,1)S(1)} %collective-permute-done.3), channel_id=1, source_target_pairs={{0,1},{1,2},{2,3},{3,4},{4,5},{5,6},{6,7},{7,8},{8,9},{9,10},{10,1... | collective-permute-start | bytes 589832 | tf_op jit(solution)/shard_map/ppermute | solution.py:85
  92.9 32.6 %collective-permute-start.5 = (bf16[384,256]{1,0:T(8,128)(2,1)S(1)}, bf16[384,256]{1,0:T(8,128)(2,1)S(1)}, u32[]{:S(2)}, u32[]{:S(2)}) collective-permute-start(bf16[384,256]{1,0:T(8,128)(2,1)S(1)} %collective-permute-done.4), channel_id=1, source_target_pairs={{0,1},{1,2},{2,3},{3,4},{4,5},{5,6},{6,7},{7,8},{8,9},{9,10},{10,1... | collective-permute-start | bytes 589832 | tf_op jit(solution)/shard_map/ppermute | solution.py:85
  125.5 12.6 %collective-permute-start.6 = (bf16[384,256]{1,0:T(8,128)(2,1)S(1)}, bf16[384,256]{1,0:T(8,128)(2,1)S(1)}, u32[]{:S(2)}, u32[]{:S(2)}) collective-permute-start(bf16[384,256]{1,0:T(8,128)(2,1)S(1)} %collective-permute-done.5), channel_id=1, source_target_pairs={{0,1},{1,2},{2,3},{3,4},{4,5},{5,6},{6,7},{7,8},{8,9},{9,10},{10,1... | collective-permute-start | bytes 589832 | tf_op jit(solution)/shard_map/ppermute | solution.py:85
  138.1 11.8 %collective-permute-start.7 = (bf16[384,256]{1,0:T(8,128)(2,1)S(1)}, bf16[384,256]{1,0:T(8,128)(2,1)S(1)}, u32[]{:S(2)}, u32[]{:S(2)}) collective-permute-start(bf16[384,256]{1,0:T(8,128)(2,1)S(1)} %collective-permute-done.6), channel_id=1, source_target_pairs={{0,1},{1,2},{2,3},{3,4},{4,5},{5,6},{6,7},{7,8},{8,9},{9,10},{10,1... | collective-permute-start | bytes 589832 | tf_op jit(solution)/shard_map/ppermute | solution.py:85
  149.9 10.9 %collective-permute-start.8 = (bf16[384,256]{1,0:T(8,128)(2,1)S(1)}, bf16[384,256]{1,0:T(8,128)(2,1)S(1)}, u32[]{:S(2)}, u32[]{:S(2)}) collective-permute-start(bf16[384,256]{1,0:T(8,128)(2,1)S(1)} %collective-permute-done.7), channel_id=1, source_target_pairs={{0,1},{1,2},{2,3},{3,4},{4,5},{5,6},{6,7},{7,8},{8,9},{9,10},{10,1... | collective-permute-start | bytes 589832 | tf_op jit(solution)/shard_map/ppermute | solution.py:85
  160.8 10.9 %collective-permute-start.9 = (bf16[384,256]{1,0:T(8,128)(2,1)S(1)}, bf16[384,256]{1,0:T(8,128)(2,1)S(1)}, u32[]{:S(2)}, u32[]{:S(2)}) collective-permute-start(bf16[384,256]{1,0:T(8,128)(2,1)S(1)} %collective-permute-done.8), channel_id=1, source_target_pairs={{0,1},{1,2},{2,3},{3,4},{4,5},{5,6},{6,7},{7,8},{8,9},{9,10},{10,1... | collective-permute-start | bytes 589832 | tf_op jit(solution)/shard_map/ppermute | solution.py:85
  171.7 10.9 %collective-permute-start.10 = (bf16[384,256]{1,0:T(8,128)(2,1)S(1)}, bf16[384,256]{1,0:T(8,128)(2,1)S(1)}, u32[]{:S(2)}, u32[]{:S(2)}) collective-permute-start(bf16[384,256]{1,0:T(8,128)(2,1)S(1)} %collective-permute-done.9), channel_id=1, source_target_pairs={{0,1},{1,2},{2,3},{3,4},{4,5},{5,6},{6,7},{7,8},{8,9},{9,10},{10,1... | collective-permute-start | bytes 589832 | tf_op jit(solution)/shard_map/ppermute | solution.py:85
  182.5 10.9 %collective-permute-start.11 = (bf16[384,256]{1,0:T(8,128)(2,1)S(1)}, bf16[384,256]{1,0:T(8,128)(2,1)S(1)}, u32[]{:S(2)}, u32[]{:S(2)}) collective-permute-start(bf16[384,256]{1,0:T(8,128)(2,1)S(1)} %collective-permute-done.10), channel_id=1, source_target_pairs={{0,1},{1,2},{2,3},{3,4},{4,5},{5,6},{6,7},{7,8},{8,9},{9,10},{10,1... | collective-permute-start | bytes 589832 | tf_op jit(solution)/shard_map/ppermute | solution.py:85
  184.5 42.5 %copy-start.9 = (f32[64]{0:T(128)}, f32[64]{0:T(128)S(1)}, u32[]{:S(2)}) copy-start(f32[64]{0:T(128)S(1)} %multiply_exponential_fusion) | copy-start | bytes 772
  193.4 10.9 %collective-permute-start.12 = (bf16[384,256]{1,0:T(8,128)(2,1)S(1)}, bf16[384,256]{1,0:T(8,128)(2,1)S(1)}, u32[]{:S(2)}, u32[]{:S(2)}) collective-permute-start(bf16[384,256]{1,0:T(8,128)(2,1)S(1)} %collective-permute-done.11), channel_id=1, source_target_pairs={{0,1},{1,2},{2,3},{3,4},{4,5},{5,6},{6,7},{7,8},{8,9},{9,10},{10,1... | collective-permute-start | bytes 589832 | tf_op jit(solution)/shard_map/ppermute | solution.py:85
  204.3 11.0 %collective-permute-start.13 = (bf16[384,256]{1,0:T(8,128)(2,1)S(1)}, bf16[384,256]{1,0:T(8,128)(2,1)S(1)}, u32[]{:S(2)}, u32[]{:S(2)}) collective-permute-start(bf16[384,256]{1,0:T(8,128)(2,1)S(1)} %collective-permute-done.12), channel_id=1, source_target_pairs={{0,1},{1,2},{2,3},{3,4},{4,5},{5,6},{6,7},{7,8},{8,9},{9,10},{10,1... | collective-permute-start | bytes 589832 | tf_op jit(solution)/shard_map/ppermute | solution.py:85
  215.3 10.9 %collective-permute-start.14 = (bf16[384,256]{1,0:T(8,128)(2,1)S(1)}, bf16[384,256]{1,0:T(8,128)(2,1)S(1)}, u32[]{:S(2)}, u32[]{:S(2)}) collective-permute-start(bf16[384,256]{1,0:T(8,128)(2,1)S(1)} %collective-permute-done.13), channel_id=1, source_target_pairs={{0,1},{1,2},{2,3},{3,4},{4,5},{5,6},{6,7},{7,8},{8,9},{9,10},{10,1... | collective-permute-start | bytes 589832 | tf_op jit(solution)/shard_map/ppermute | solution.py:85
  217.3 15.2 %copy-start.7 = (f32[384,4]{0,1:T(4,128)}, f32[384,4]{0,1:T(4,128)S(1)}, u32[]{:S(2)}) copy-start(f32[384,4]{0,1:T(4,128)S(1)} %get-tuple-element.17) | copy-start | bytes 18436
  226.9 76.5 %copy-start.4 = (bf16[4,16,256]{2,1,0:T(8,128)(2,1)S(1)}, bf16[4,16,256]{2,1,0:T(8,128)(2,1)}, u32[]{:S(2)}) copy-start(bf16[4,16,256]{2,1,0:T(8,128)(2,1)} %gather_fusion.3) | copy-start | bytes 98308
  313.6 6.4 %copy-start.10 = (f32[128]{0:T(128)S(1)}, f32[128]{0:T(128)}, u32[]{:S(2)}) copy-start(f32[128]{0:T(128)} %convert_element_type.112) | copy-start | bytes 1540
  313.6 6.8 %copy-start.2 = (pred[384,896]{0,1:T(8,128)(4,1)S(1)}, pred[384,896]{0,1:T(8,128)(4,1)}, u32[]{:S(2)}) copy-start(pred[384,896]{0,1:T(8,128)(4,1)} %pad_add_fusion) | copy-start | bytes 1032196
  313.6 6.8 %copy-start.3 = (bf16[512,1,128]{2,0,1:T(8,128)(2,1)S(1)}, bf16[512,1,128]{2,0,1:T(8,128)(2,1)}, u32[]{:S(2)}) copy-start(bf16[512,1,128]{2,0,1:T(8,128)(2,1)} %copy.67) | copy-start | bytes 393220
  322.2 4.4 copy-start.5
  322.2 33.6 %copy-start.6 = (bf16[2,16,256]{2,1,0:T(8,128)(2,1)S(1)}, bf16[2,16,256]{2,1,0:T(8,128)(2,1)}, u32[]{:S(2)}) copy-start(bf16[2,16,256]{2,1,0:T(8,128)(2,1)} %param.31) | copy-start | bytes 49156
  322.3 63.8 %copy-start.8 = (f32[384,4]{0,1:T(4,128)S(1)}, f32[384,4]{0,1:T(4,128)}, u32[]{:S(2)}) copy-start(f32[384,4]{0,1:T(4,128)} %copy-done.7) | copy-start | bytes 18436
Sparse Core Ops, SparseCore 0:
  10.1 75.3 all-gather.6
  88.3 68.7 all-gather.4
  159.2 68.8 all-gather.8
  230.0 70.6 all-gather.10
  326.7 83.1 reduce-scatter.1
